TPU v7x, 32 devices: a whole 2x2x4 slice. The times are simulated.
32 devices in a mesh: parts: 32 (over z, y, x, core).
Axes of the slice: x: 2, y: 2, z: 4, core: 2. Of those that a mesh axis runs over, the one named last changes fastest.
Arguments:
- basis: float32 [16, 32768], P(None, 'parts'), may hold values from -8000 to 8000, as said below
- k_tiles: float32 [256, 5, 128, 128], P('parts'), may hold values from -3 to 11, as said below
- m_tiles: float32 [256, 5, 128, 128], P('parts'), may hold values from -2 to 4, as said below
- tile_part: int32 [256, 5], P('parts'), may hold values from 0 to 31, as said below
- tile_slot: int32 [256, 5], P('parts'), may hold values from 0 to 7, as said below
- iface_rows: int32 [64], P('parts'), may hold values from 0 to 7
Outputs:
- corrections: float32 [16, 32768], P(None, 'parts')
- theta: float32 [16], replicated
Inputs may be any that keep to these rules, and one draw needn't show every extreme that they name: `basis`: the rows form a full-rank set. `k_tiles`: block 0 of every row tile has a positive diagonal well above its other entries. `m_tiles`: block 0 of every row tile has a positive diagonal. `tile_part`: block 0 of a row tile lies in its own partition; every other block lies in its own partition, in the partition 1 away on either side, or in the partition 16 away, counted modulo the number of partitions. `tile_slot`: where the block lies in the own partition this is a row tile of it (for block 0 the row tile itself); elsewhere an interface slot below 2.
All inputs are finite; a program needn't handle non-finite values.
Results may differ from a plain program's by a relative error of at most 0.0003.
Values sent between devices are 32-bit elements; how exact they have to be, the bound alone decides.
No kernel may reach another device: no remote copies, remote signals or barrier semaphores. Data moves between devices by JAX's collectives and lax.ppermute only.
A program may use at most 64 MiB of HBM per device.

v0:
```python
import jax
import jax.numpy as jnp
from jax import lax
from jax.sharding import PartitionSpec as P

STEPS = 4
relax = 0.4


def shifted(value, axis, steps):
    count = lax.axis_size(axis)
    pairs = [(source, (source + steps) % count) for source in range(count)]
    return lax.ppermute(value, axis, pairs)


def product(left, right):
    return jnp.dot(left, right, precision=lax.Precision.HIGHEST, preferred_element_type=jnp.float32)


def inverse_lower(chol):
    eye = jnp.eye(chol.shape[0], dtype=chol.dtype)
    return jax.scipy.linalg.solve_triangular(chol, eye, lower=True)


def shards(basis, k_tiles, m_tiles, tile_part, tile_slot, iface_rows):
    pairs = basis.shape[0]
    tiles = k_tiles.shape[0]
    width = k_tiles.shape[2]
    count = iface_rows.shape[0]
    parts = lax.axis_size("parts")
    me = lax.axis_index("parts")
    scale = 1.0 / (basis.shape[1] * parts)
    far_step = parts // 2
    neighbours = (1, -1, far_step, -far_step)
    direction = jnp.full_like(tile_part, 3)
    for number in (2, 1, 0):
        target = (me + neighbours[number] + parts) % parts
        direction = jnp.where(tile_part == target, number, direction)
    remote = tiles + direction * count + tile_slot
    columns = jnp.where(tile_part == me, tile_slot, remote)

    def apply_pair(vectors):
        blocks = vectors.reshape(pairs, tiles, width)
        outgoing = jnp.take(blocks, iface_rows, axis=1)
        received = []
        for offset in neighbours:
            received.append(shifted(outgoing, "parts", -offset))
        incoming = jnp.concatenate(received, axis=1)
        sources = jnp.concatenate([blocks, incoming], axis=1)
        picked = jnp.take(sources, columns, axis=1)
        stiff = jnp.einsum("ptbc,tbrc->ptr", picked, k_tiles, precision=lax.Precision.HIGHEST)
        mass = jnp.einsum("ptbc,tbrc->ptr", picked, m_tiles, precision=lax.Precision.HIGHEST)
        return (stiff.reshape(pairs, -1), mass.reshape(pairs, -1))

    gram = lax.psum(product(basis, basis.T) * scale, "parts")
    inv_v = inverse_lower(jnp.linalg.cholesky(gram))
    ortho = product(inv_v, basis)
    k_ortho, m_ortho = apply_pair(ortho)
    mass_gram, stiff_cross = lax.psum(
        (product(m_ortho, m_ortho.T) * scale, product(m_ortho, k_ortho.T) * scale), "parts"
    )
    chol_b = jnp.linalg.cholesky(mass_gram)
    inv_b = inverse_lower(chol_b)
    test_basis = product(inv_b, m_ortho)
    projected_k = product(inv_b, stiff_cross)
    theta = jnp.diagonal(projected_k) / jnp.diagonal(chol_b)
    resid = k_ortho - theta[:, None] * m_ortho
    diag_k = jnp.diagonal(k_tiles[:, 0], axis1=1, axis2=2).reshape(-1)
    correct = -relax * resid / diag_k
    for step in range(STEPS):
        right = lax.psum(product(correct, ortho.T) * scale, "parts")
        moved = correct - product(right, ortho)
        k_moved, m_moved = apply_pair(moved)
        image = k_moved - theta[:, None] * m_moved
        left = lax.psum(product(image, test_basis.T) * scale, "parts")
        image = image - product(left, test_basis)
        correct = correct - relax * (resid + image) / diag_k
    final = lax.psum(product(correct, ortho.T) * scale, "parts")
    correct = correct - product(final, ortho)
    return (correct, theta)


def solution(mesh):
    placed = (
        P(None, "parts"),
        P("parts", None, None, None),
        P("parts", None, None, None),
        P("parts", None),
        P("parts", None),
        P("parts"),
    )
    return jax.shard_map(
        shards, mesh=mesh, in_specs=placed, out_specs=(P(None, "parts"), P()), check_vma=False
    )
```

profile of v0, /device:TPU:0, one launch (start us, length us, event | category | flops | bytes accessed | tf_op | source)
XLA Modules:
  0.0 536.0 jit_solution(4131112549924731336)
XLA Ops:
  0.6 0.8 compare_select_fusion.1
  2.1 1.1 convolution_multiply_fusion.9
  3.2 42.1 %psum.84 = f32[16,16]{0,1:T(8,128)S(1)} all-reduce(f32[16,16]{0,1:T(8,128)S(1)} %convolution_multiply_fusion.9), channel_id=1, replica_groups=mesh['parts'=32] {'parts'}, use_global_device_ids=true, to_apply=%region_0.1 | all-reduce | flops 256 | bytes 2048 | tf_op jit(solution)/shard_map/psum | solution.py:55
  45.3 1.5 cholesky.44
  48.1 1.2 custom-call.12
  49.6 1.0 fusion.99
  51.3 2.5 collective-permute-start
  53.8 0.8 collective-permute-start.2
  54.6 0.7 compare_and_fusion
  55.4 1.1 slice.11
  56.5 4.6 copy.65
  61.1 1.8 gather_fusion.2
  63.6 4.3 fusion.32
  68.0 2.6 fusion.30
  71.0 40.2 %all-reduce = (f32[16,16]{0,1:T(8,128)S(1)}, f32[16,16]{0,1:T(8,128)S(1)}) all-reduce(f32[16,16]{0,1:T(8,128)S(1)} %fusion.21, f32[16,16]{0,1:T(8,128)S(1)} %fusion.20), channel_id=1, replica_groups=mesh['parts'=32] {'parts'}, use_global_device_ids=true, to_apply=%region_3.8 | all-reduce | flops 512 | bytes 4096 | tf_op jit(solution)/shard_map/psum | solution.py:59
  111.3 1.5 cholesky.55
  114.1 1.2 custom-call.13
  115.9 0.7 gather_fusion
  117.5 39.9 %psum.87 = f32[16,16]{0,1:T(8,128)S(1)} all-reduce(f32[16,16]{0,1:T(8,128)S(1)} %convolution_multiply_fusion.8), channel_id=1, replica_groups=mesh['parts'=32] {'parts'}, use_global_device_ids=true, to_apply=%region_5.10 | all-reduce | flops 256 | bytes 2048 | tf_op jit(solution)/shard_map/psum | solution.py:71
  158.3 2.2 collective-permute-start.3
  160.7 1.8 collective-permute-start.5
  162.5 5.0 collective-permute-done.4
  168.1 2.6 convolution_bitcast_fusion.6
  170.8 2.6 convolution_bitcast_fusion.7
  173.7 36.9 %psum.88 = f32[16,16]{0,1:T(8,128)S(1)} all-reduce(f32[16,16]{0,1:T(8,128)S(1)} %convolution_multiply_fusion.7), channel_id=1, replica_groups=mesh['parts'=32] {'parts'}, use_global_device_ids=true, to_apply=%region_6.11 | all-reduce | flops 256 | bytes 2048 | tf_op jit(solution)/shard_map/psum | solution.py:75
  211.0 41.0 %psum.89 = f32[16,16]{0,1:T(8,128)S(1)} all-reduce(f32[16,16]{0,1:T(8,128)S(1)} %convolution_multiply_fusion.6), channel_id=1, replica_groups=mesh['parts'=32] {'parts'}, use_global_device_ids=true, to_apply=%region_7.12 | all-reduce | flops 256 | bytes 2048 | tf_op jit(solution)/shard_map/psum | solution.py:71
  252.9 1.8 collective-permute-start.6
  255.2 1.0 collective-permute-done.6
  256.2 5.3 collective-permute-done.7
  262.2 2.6 convolution_bitcast_fusion.4
  264.8 2.6 convolution_bitcast_fusion.5
  267.7 37.4 %psum.90 = f32[16,16]{0,1:T(8,128)S(1)} all-reduce(f32[16,16]{0,1:T(8,128)S(1)} %convolution_multiply_fusion.5), channel_id=1, replica_groups=mesh['parts'=32] {'parts'}, use_global_device_ids=true, to_apply=%region_8.13 | all-reduce | flops 256 | bytes 2048 | tf_op jit(solution)/shard_map/psum | solution.py:75
  305.5 41.0 %psum.91 = f32[16,16]{0,1:T(8,128)S(1)} all-reduce(f32[16,16]{0,1:T(8,128)S(1)} %convolution_multiply_fusion.4), channel_id=1, replica_groups=mesh['parts'=32] {'parts'}, use_global_device_ids=true, to_apply=%region_9.14 | all-reduce | flops 256 | bytes 2048 | tf_op jit(solution)/shard_map/psum | solution.py:71
  347.5 1.9 collective-permute-start.9
  349.5 1.4 collective-permute-done.9
  350.8 5.3 collective-permute-done.10
  356.8 2.6 convolution_bitcast_fusion.2
  359.4 2.6 convolution_bitcast_fusion.3
  362.3 36.9 %psum.92 = f32[16,16]{0,1:T(8,128)S(1)} all-reduce(f32[16,16]{0,1:T(8,128)S(1)} %convolution_multiply_fusion.3), channel_id=1, replica_groups=mesh['parts'=32] {'parts'}, use_global_device_ids=true, to_apply=%region_10.15 | all-reduce | flops 256 | bytes 2048 | tf_op jit(solution)/shard_map/psum | solution.py:75
  399.7 41.0 %psum.93 = f32[16,16]{0,1:T(8,128)S(1)} all-reduce(f32[16,16]{0,1:T(8,128)S(1)} %convolution_multiply_fusion.2), channel_id=1, replica_groups=mesh['parts'=32] {'parts'}, use_global_device_ids=true, to_apply=%region_11.16 | all-reduce | flops 256 | bytes 2048 | tf_op jit(solution)/shard_map/psum | solution.py:71
  441.6 1.9 collective-permute-start.12
  443.7 1.2 collective-permute-done.12
  444.9 5.5 %collective-permute-done.13 = f32[16,2,128]{2,0,1:T(8,128)S(1)} collective-permute-done((f32[16,2,128]{2,0,1:T(8,128)S(1)}, f32[16,2,128]{2,0,1:T(8,128)S(1)}, u32[]{:S(2)}, u32[]{:S(2)}) %collective-permute-start.13) | collective-permute-done | bytes 16416 | tf_op jit(solution)/shard_map/ppermute | solution.py:13
  451.0 2.6 convolution_bitcast_fusion
  453.7 2.6 convolution_bitcast_fusion.1
  456.6 36.9 %psum.94 = f32[16,16]{0,1:T(8,128)S(1)} all-reduce(f32[16,16]{0,1:T(8,128)S(1)} %convolution_multiply_fusion.1), channel_id=1, replica_groups=mesh['parts'=32] {'parts'}, use_global_device_ids=true, to_apply=%region_12.17 | all-reduce | flops 256 | bytes 2048 | tf_op jit(solution)/shard_map/psum | solution.py:75
  493.9 41.0 %psum.95 = f32[16,16]{0,1:T(8,128)S(1)} all-reduce(f32[16,16]{0,1:T(8,128)S(1)} %convolution_multiply_fusion), channel_id=1, replica_groups=mesh['parts'=32] {'parts'}, use_global_device_ids=true, to_apply=%region_13.18 | all-reduce | flops 256 | bytes 2048 | tf_op jit(solution)/shard_map/psum | solution.py:78
  535.0 0.9 convolution_subtract_fusion
  (116 shorter events, 16.9 us)
Async XLA Ops:
  0.6 67.4 %copy-start = (f32[8,5,128,128]{3,2,1,0:T(8,128)S(1)}, f32[8,5,128,128]{3,2,1,0:T(8,128)}, u32[]{:S(2)}) copy-start(f32[8,5,128,128]{3,2,1,0:T(8,128)} %param.15) | copy-start | bytes 7864324
  51.3 11.7 %collective-permute-start = (f32[16,2,128]{2,0,1:T(8,128)S(1)}, f32[16,2,128]{2,0,1:T(8,128)S(1)}, u32[]{:S(2)}, u32[]{:S(2)}) collective-permute-start(f32[16,2,128]{2,0,1:T(8,128)S(1)} %select_bitcast_fusion.4), channel_id=1, source_target_pairs={{0,31},{1,0},{2,1},{3,2},{4,3},{5,4},{6,5},{7,6},{8,7},{9,8},{10,9... | collective-permute-start | bytes 49160 | tf_op jit(solution)/shard_map/ppermute | solution.py:13
  53.8 9.2 %collective-permute-start.1 = (f32[16,2,128]{2,0,1:T(8,128)S(1)}, f32[16,2,128]{2,0,1:T(8,128)S(1)}, u32[]{:S(2)}, u32[]{:S(2)}) collective-permute-start(f32[16,2,128]{2,0,1:T(8,128)S(1)} %select_bitcast_fusion.4), channel_id=1, source_target_pairs={{0,1},{1,2},{2,3},{3,4},{4,5},{5,6},{6,7},{7,8},{8,9},{9,10},{10,1... | collective-permute-start | bytes 49160 | tf_op jit(solution)/shard_map/ppermute | solution.py:13
  53.8 9.2 %collective-permute-start.2 = (f32[16,2,128]{2,0,1:T(8,128)S(1)}, f32[16,2,128]{2,0,1:T(8,128)S(1)}, u32[]{:S(2)}, u32[]{:S(2)}) collective-permute-start(f32[16,2,128]{2,0,1:T(8,128)S(1)} %select_bitcast_fusion.4), channel_id=1, source_target_pairs={{0,16},{1,17},{2,18},{3,19},{4,20},{5,21},{6,22},{7,23},{8,24},{9,... | collective-permute-start | bytes 49160 | tf_op jit(solution)/shard_map/ppermute | solution.py:13
  117.2 376.2 %copy-start.5 = (f32[16]{0:T(128)}, f32[16]{0:T(128)S(1)}, u32[]{:S(2)}) copy-start(f32[16]{0:T(128)S(1)} %div.47) | copy-start | bytes 196
  158.3 4.2 collective-permute-start.3
  160.5 7.0 %collective-permute-start.4 = (f32[16,2,128]{2,0,1:T(8,128)S(1)}, f32[16,2,128]{2,0,1:T(8,128)S(1)}, u32[]{:S(2)}, u32[]{:S(2)}) collective-permute-start(f32[16,2,128]{2,0,1:T(8,128)S(1)} %select_bitcast_fusion.3), channel_id=1, source_target_pairs={{0,1},{1,2},{2,3},{3,4},{4,5},{5,6},{6,7},{7,8},{8,9},{9,10},{10,1... | collective-permute-start | bytes 49160 | tf_op jit(solution)/shard_map/ppermute | solution.py:13
  160.7 6.8 %collective-permute-start.5 = (f32[16,2,128]{2,0,1:T(8,128)S(1)}, f32[16,2,128]{2,0,1:T(8,128)S(1)}, u32[]{:S(2)}, u32[]{:S(2)}) collective-permute-start(f32[16,2,128]{2,0,1:T(8,128)S(1)} %select_bitcast_fusion.3), channel_id=1, source_target_pairs={{0,16},{1,17},{2,18},{3,19},{4,20},{5,21},{6,22},{7,23},{8,24},{9,... | collective-permute-start | bytes 49160 | tf_op jit(solution)/shard_map/ppermute | solution.py:13
  168.1 2.6 copy-start.1
  252.9 3.3 collective-permute-start.6
  254.8 6.8 %collective-permute-start.7 = (f32[16,2,128]{2,0,1:T(8,128)S(1)}, f32[16,2,128]{2,0,1:T(8,128)S(1)}, u32[]{:S(2)}, u32[]{:S(2)}) collective-permute-start(f32[16,2,128]{2,0,1:T(8,128)S(1)} %select_bitcast_fusion.2), channel_id=1, source_target_pairs={{0,1},{1,2},{2,3},{3,4},{4,5},{5,6},{6,7},{7,8},{8,9},{9,10},{10,1... | collective-permute-start | bytes 49160 | tf_op jit(solution)/shard_map/ppermute | solution.py:13
  254.8 6.8 %collective-permute-start.8 = (f32[16,2,128]{2,0,1:T(8,128)S(1)}, f32[16,2,128]{2,0,1:T(8,128)S(1)}, u32[]{:S(2)}, u32[]{:S(2)}) collective-permute-start(f32[16,2,128]{2,0,1:T(8,128)S(1)} %select_bitcast_fusion.2), channel_id=1, source_target_pairs={{0,16},{1,17},{2,18},{3,19},{4,20},{5,21},{6,22},{7,23},{8,24},{9,... | collective-permute-start | bytes 49160 | tf_op jit(solution)/shard_map/ppermute | solution.py:13
  262.2 2.6 copy-start.2
  347.5 3.3 collective-permute-start.9
  349.4 6.8 %collective-permute-start.10 = (f32[16,2,128]{2,0,1:T(8,128)S(1)}, f32[16,2,128]{2,0,1:T(8,128)S(1)}, u32[]{:S(2)}, u32[]{:S(2)}) collective-permute-start(f32[16,2,128]{2,0,1:T(8,128)S(1)} %select_bitcast_fusion.1), channel_id=1, source_target_pairs={{0,1},{1,2},{2,3},{3,4},{4,5},{5,6},{6,7},{7,8},{8,9},{9,10},{10,1... | collective-permute-start | bytes 49160 | tf_op jit(solution)/shard_map/ppermute | solution.py:13
  349.4 6.8 %collective-permute-start.11 = (f32[16,2,128]{2,0,1:T(8,128)S(1)}, f32[16,2,128]{2,0,1:T(8,128)S(1)}, u32[]{:S(2)}, u32[]{:S(2)}) collective-permute-start(f32[16,2,128]{2,0,1:T(8,128)S(1)} %select_bitcast_fusion.1), channel_id=1, source_target_pairs={{0,16},{1,17},{2,18},{3,19},{4,20},{5,21},{6,22},{7,23},{8,24},{9,... | collective-permute-start | bytes 49160 | tf_op jit(solution)/shard_map/ppermute | solution.py:13
  356.8 2.6 copy-start.3
  441.6 3.3 collective-permute-start.12
  443.5 6.9 %collective-permute-start.13 = (f32[16,2,128]{2,0,1:T(8,128)S(1)}, f32[16,2,128]{2,0,1:T(8,128)S(1)}, u32[]{:S(2)}, u32[]{:S(2)}) collective-permute-start(f32[16,2,128]{2,0,1:T(8,128)S(1)} %select_bitcast_fusion), channel_id=1, source_target_pairs={{0,1},{1,2},{2,3},{3,4},{4,5},{5,6},{6,7},{7,8},{8,9},{9,10},{10,1... | collective-permute-start | bytes 49160 | tf_op jit(solution)/shard_map/ppermute | solution.py:13
  443.7 6.8 %collective-permute-start.14 = (f32[16,2,128]{2,0,1:T(8,128)S(1)}, f32[16,2,128]{2,0,1:T(8,128)S(1)}, u32[]{:S(2)}, u32[]{:S(2)}) collective-permute-start(f32[16,2,128]{2,0,1:T(8,128)S(1)} %select_bitcast_fusion), channel_id=1, source_target_pairs={{0,16},{1,17},{2,18},{3,19},{4,20},{5,21},{6,22},{7,23},{8,24},{9,... | collective-permute-start | bytes 49160 | tf_op jit(solution)/shard_map/ppermute | solution.py:13
  451.0 2.6 copy-start.4
where the time goes:
time: 545 us; the launch traced here: 536 us
  blocking collectives  434 us (80%)
  matrix products  36.2 us (7%)
  waiting for transfers between devices  24.7 us (5%)
  local copies, waits for them, and re-layouts  15 us (3%)
  starting transfers between devices  13.8 us (3%)
  other arithmetic  10.7 us (2%)
    psum x4, blocking collectives, shards(): right = lax.psum(product(correct, ortho.T) * scale, 'parts')  163 us
    psum x4, blocking collectives, shards(): left = lax.psum(product(image, test_basis.T) * scale, 'parts')  148 us
    psum x1, blocking collectives, shards(): gram = lax.psum(product(basis, basis.T) * scale, 'parts')  42.1 us
    psum x1, blocking collectives, shards(): final = lax.psum(product(correct, ortho.T) * scale, 'parts')  41 us
    psum x1, blocking collectives, shards(): lax.psum((product(m_ortho, m_ortho.T) * scale, product(m_ortho, k_ortho.T...  40.2 us
    ppermute x15, waiting for transfers between devices, shifted(): return lax.ppermute(value, axis, pairs)  24.7 us
    dot_general x5, matrix products, apply_pair(): jnp.einsum('ptbc,tbrc->ptr', picked, k_tiles, precision=lax.Precision.HIG...  14.9 us
    ppermute x15, starting transfers between devices, shifted(): return lax.ppermute(value, axis, pairs)  13.8 us
  transfers between devices with their start and end apart: 15, of which 7 were waited for; matrix products, arithmetic and copies ran while one was open for 2% of the time, Pallas kernels for 0%

commit v1 on v0

--- a/solution.py
+++ b/solution.py
@@ -72,7 +72,8 @@
         moved = correct - product(right, ortho)
         k_moved, m_moved = apply_pair(moved)
         image = k_moved - theta[:, None] * m_moved
-        left = lax.psum(product(image, test_basis.T) * scale, "parts")
+        xin = product(image, test_basis.T) * scale
+        left = jnp.sum(lax.all_gather(xin, "parts"), axis=0)
         image = image - product(left, test_basis)
         correct = correct - relax * (resid + image) / diag_k
     final = lax.psum(product(correct, ortho.T) * scale, "parts")

time: 545 us -> 526 us (0.965); the launches traced: 536 us -> 524 us
  blocking collectives: 434 us -> 420 us
  starting transfers between devices: 13.8 us -> 21.3 us
  waiting for transfers between devices: 24.7 us -> 19 us
    all_gather x0 -> x4, blocking collectives: none -> 150 us  [shards(): left = jnp.sum(lax.all_gather(xin, 'parts'), axis=0)]
    psum x4 -> x0, blocking collectives: 148 us -> none  [shards(): left = lax.psum(product(image, test_basis.T) * scale, 'parts')]
    psum x4, blocking collectives: 163 us -> 151 us  [shards(): right = lax.psum(product(correct, ortho.T) * scale, 'parts')]
    ppermute x15, starting transfers between devices: 13.8 us -> 21.3 us  [shifted(): return lax.ppermute(value, axis, pairs)]
    ppermute x15, waiting for transfers between devices: 24.7 us -> 19 us  [shifted(): return lax.ppermute(value, axis, pairs)]
  transfers between devices with their start and end apart: 15 -> 15, of which waited for: 7 -> 4; matrix products, arithmetic and copies ran while one was open for 2% -> 2% of each run, Pallas kernels for 0% -> 0%
where the time goes in v1:
time: 526 us; the launch traced here: 524 us
  blocking collectives  420 us (80%)
  matrix products  36 us (7%)
  starting transfers between devices  21.3 us (4%)
  waiting for transfers between devices  19 us (4%)
  local copies, waits for them, and re-layouts  15.3 us (3%)
  other arithmetic  10.9 us (2%)
    psum x4, blocking collectives, shards(): right = lax.psum(product(correct, ortho.T) * scale, 'parts')  151 us
    all_gather x4, blocking collectives, shards(): left = jnp.sum(lax.all_gather(xin, 'parts'), axis=0)  150 us
    psum x1, blocking collectives, shards(): gram = lax.psum(product(basis, basis.T) * scale, 'parts')  42.1 us
    psum x1, blocking collectives, shards(): lax.psum((product(m_ortho, m_ortho.T) * scale, product(m_ortho, k_ortho.T...  40.2 us
    psum x1, blocking collectives, shards(): final = lax.psum(product(correct, ortho.T) * scale, 'parts')  36.9 us
    ppermute x15, starting transfers between devices, shifted(): return lax.ppermute(value, axis, pairs)  21.3 us
    ppermute x15, waiting for transfers between devices, shifted(): return lax.ppermute(value, axis, pairs)  19 us
    dot_general x5, matrix products, apply_pair(): jnp.einsum('ptbc,tbrc->ptr', picked, k_tiles, precision=lax.Precision.HIG...  14.9 us
  transfers between devices with their start and end apart: 15, of which 4 were waited for; matrix products, arithmetic and copies ran while one was open for 2% of the time, Pallas kernels for 0%

profile of v1, /device:TPU:0, one launch (start us, length us, event | category | flops | bytes accessed | tf_op | source)
XLA Modules:
  0.0 524.1 jit_solution(6854986814906240511)
XLA Ops:
  0.6 0.8 compare_select_fusion.1
  2.1 1.1 convolution_multiply_fusion.9
  3.2 42.1 %psum.56 = f32[16,16]{0,1:T(8,128)S(1)} all-reduce(f32[16,16]{0,1:T(8,128)S(1)} %convolution_multiply_fusion.9), channel_id=1, replica_groups=mesh['parts'=32] {'parts'}, use_global_device_ids=true, to_apply=%region_0.1 | all-reduce | flops 256 | bytes 2048 | tf_op jit(solution)/shard_map/psum | solution.py:55
  45.3 1.5 cholesky.44
  48.1 1.2 custom-call.12
  49.6 1.0 fusion.99
  51.3 2.5 collective-permute-start
  53.8 0.8 collective-permute-start.2
  54.6 0.7 compare_and_fusion
  55.4 1.1 slice.11
  56.5 4.6 copy.136
  61.1 1.8 gather_fusion.2
  63.6 4.3 fusion.32
  68.0 2.6 fusion.30
  71.0 40.2 %all-reduce = (f32[16,16]{0,1:T(8,128)S(1)}, f32[16,16]{0,1:T(8,128)S(1)}) all-reduce(f32[16,16]{0,1:T(8,128)S(1)} %fusion.21, f32[16,16]{0,1:T(8,128)S(1)} %fusion.20), channel_id=1, replica_groups=mesh['parts'=32] {'parts'}, use_global_device_ids=true, to_apply=%region_3.8 | all-reduce | flops 512 | bytes 4096 | tf_op jit(solution)/shard_map/psum | solution.py:59
  111.3 1.5 cholesky.55
  114.1 1.2 custom-call.13
  115.9 0.7 gather_fusion
  117.5 39.9 %psum.59 = f32[16,16]{0,1:T(8,128)S(1)} all-reduce(f32[16,16]{0,1:T(8,128)S(1)} %convolution_multiply_fusion.8), channel_id=1, replica_groups=mesh['parts'=32] {'parts'}, use_global_device_ids=true, to_apply=%region_5.10 | all-reduce | flops 256 | bytes 2048 | tf_op jit(solution)/shard_map/psum | solution.py:71
  158.3 2.2 collective-permute-start.3
  160.5 1.8 collective-permute-start.5
  162.3 5.0 collective-permute-done.4
  167.9 2.6 convolution_bitcast_fusion.6
  170.5 2.7 convolution_bitcast_fusion.7
  173.5 37.1 %all-gather = f32[512,16]{1,0:T(8,128)S(1)} all-gather(f32[16,16]{1,0:T(8,128)S(1)} %copy.77), channel_id=2, replica_groups=mesh['parts'=32] {'parts'}, dimensions={0}, use_global_device_ids=true | all-gather | bytes 33792 | tf_op jit(solution)/shard_map/all_gather | solution.py:76
  211.0 37.3 %psum.60 = f32[16,16]{0,1:T(8,128)S(1)} all-reduce(f32[16,16]{0,1:T(8,128)S(1)} %convolution_multiply_fusion.6), channel_id=1, replica_groups=mesh['parts'=32] {'parts'}, use_global_device_ids=true, to_apply=%region_7.12 | all-reduce | flops 256 | bytes 2048 | tf_op jit(solution)/shard_map/psum | solution.py:71
  249.2 2.6 collective-permute-start.6
  251.8 2.0 collective-permute-start.8
  253.8 4.7 collective-permute-done.7
  259.2 2.6 convolution_bitcast_fusion.4
  261.8 2.7 convolution_bitcast_fusion.5
  264.9 37.8 %all-gather.1 = f32[512,16]{1,0:T(8,128)S(1)} all-gather(f32[16,16]{1,0:T(8,128)S(1)} %copy.85), channel_id=3, replica_groups=mesh['parts'=32] {'parts'}, dimensions={0}, use_global_device_ids=true | all-gather | bytes 33792 | tf_op jit(solution)/shard_map/all_gather | solution.py:76
  303.1 37.1 %psum.61 = f32[16,16]{0,1:T(8,128)S(1)} all-reduce(f32[16,16]{0,1:T(8,128)S(1)} %convolution_multiply_fusion.4), channel_id=1, replica_groups=mesh['parts'=32] {'parts'}, use_global_device_ids=true, to_apply=%region_9.14 | all-reduce | flops 256 | bytes 2048 | tf_op jit(solution)/shard_map/psum | solution.py:71
  341.1 2.6 collective-permute-start.9
  343.7 2.1 collective-permute-start.11
  345.9 4.6 collective-permute-done.10
  351.1 2.6 convolution_bitcast_fusion.2
  353.8 2.7 convolution_bitcast_fusion.3
  356.8 37.5 %all-gather.2 = f32[512,16]{1,0:T(8,128)S(1)} all-gather(f32[16,16]{1,0:T(8,128)S(1)} %copy.93), channel_id=4, replica_groups=mesh['parts'=32] {'parts'}, dimensions={0}, use_global_device_ids=true | all-gather | bytes 33792 | tf_op jit(solution)/shard_map/all_gather | solution.py:76
  394.7 36.9 %psum.62 = f32[16,16]{0,1:T(8,128)S(1)} all-reduce(f32[16,16]{0,1:T(8,128)S(1)} %convolution_multiply_fusion.2), channel_id=1, replica_groups=mesh['parts'=32] {'parts'}, use_global_device_ids=true, to_apply=%region_11.16 | all-reduce | flops 256 | bytes 2048 | tf_op jit(solution)/shard_map/psum | solution.py:71
  432.5 2.6 collective-permute-start.12
  435.1 2.1 collective-permute-start.14
  437.2 4.6 collective-permute-done.13
  442.5 2.6 convolution_bitcast_fusion
  445.1 2.7 convolution_bitcast_fusion.1
  448.2 37.8 %all-gather.3 = f32[512,16]{1,0:T(8,128)S(1)} all-gather(f32[16,16]{1,0:T(8,128)S(1)} %copy.101), channel_id=5, replica_groups=mesh['parts'=32] {'parts'}, dimensions={0}, use_global_device_ids=true | all-gather | bytes 33792 | tf_op jit(solution)/shard_map/all_gather | solution.py:76
  486.4 36.9 %psum.63 = f32[16,16]{0,1:T(8,128)S(1)} all-reduce(f32[16,16]{0,1:T(8,128)S(1)} %convolution_multiply_fusion), channel_id=1, replica_groups=mesh['parts'=32] {'parts'}, use_global_device_ids=true, to_apply=%region_13.18 | all-reduce | flops 256 | bytes 2048 | tf_op jit(solution)/shard_map/psum | solution.py:79
  523.2 0.9 convolution_subtract_fusion
  (124 shorter events, 16.2 us)
Async XLA Ops:
  0.6 67.3 %copy-start = (f32[8,5,128,128]{3,2,1,0:T(8,128)S(1)}, f32[8,5,128,128]{3,2,1,0:T(8,128)}, u32[]{:S(2)}) copy-start(f32[8,5,128,128]{3,2,1,0:T(8,128)} %param.15) | copy-start | bytes 7864324
  51.3 11.7 %collective-permute-start = (f32[16,2,128]{2,0,1:T(8,128)S(1)}, f32[16,2,128]{2,0,1:T(8,128)S(1)}, u32[]{:S(2)}, u32[]{:S(2)}) collective-permute-start(f32[16,2,128]{2,0,1:T(8,128)S(1)} %select_bitcast_fusion.4), channel_id=1, source_target_pairs={{0,31},{1,0},{2,1},{3,2},{4,3},{5,4},{6,5},{7,6},{8,7},{9,8},{10,9... | collective-permute-start | bytes 49160 | tf_op jit(solution)/shard_map/ppermute | solution.py:13
  53.8 9.2 %collective-permute-start.1 = (f32[16,2,128]{2,0,1:T(8,128)S(1)}, f32[16,2,128]{2,0,1:T(8,128)S(1)}, u32[]{:S(2)}, u32[]{:S(2)}) collective-permute-start(f32[16,2,128]{2,0,1:T(8,128)S(1)} %select_bitcast_fusion.4), channel_id=1, source_target_pairs={{0,1},{1,2},{2,3},{3,4},{4,5},{5,6},{6,7},{7,8},{8,9},{9,10},{10,1... | collective-permute-start | bytes 49160 | tf_op jit(solution)/shard_map/ppermute | solution.py:13
  53.8 9.2 %collective-permute-start.2 = (f32[16,2,128]{2,0,1:T(8,128)S(1)}, f32[16,2,128]{2,0,1:T(8,128)S(1)}, u32[]{:S(2)}, u32[]{:S(2)}) collective-permute-start(f32[16,2,128]{2,0,1:T(8,128)S(1)} %select_bitcast_fusion.4), channel_id=1, source_target_pairs={{0,16},{1,17},{2,18},{3,19},{4,20},{5,21},{6,22},{7,23},{8,24},{9,... | collective-permute-start | bytes 49160 | tf_op jit(solution)/shard_map/ppermute | solution.py:13
  117.3 368.7 %copy-start.5 = (f32[16]{0:T(128)}, f32[16]{0:T(128)S(1)}, u32[]{:S(2)}) copy-start(f32[16]{0:T(128)S(1)} %div.47) | copy-start | bytes 196
  158.3 4.0 collective-permute-start.3
  160.5 6.8 %collective-permute-start.4 = (f32[16,2,128]{2,0,1:T(8,128)S(1)}, f32[16,2,128]{2,0,1:T(8,128)S(1)}, u32[]{:S(2)}, u32[]{:S(2)}) collective-permute-start(f32[16,2,128]{2,0,1:T(8,128)S(1)} %select_bitcast_fusion.3), channel_id=1, source_target_pairs={{0,1},{1,2},{2,3},{3,4},{4,5},{5,6},{6,7},{7,8},{8,9},{9,10},{10,1... | collective-permute-start | bytes 49160 | tf_op jit(solution)/shard_map/ppermute | solution.py:13
  160.5 6.8 %collective-permute-start.5 = (f32[16,2,128]{2,0,1:T(8,128)S(1)}, f32[16,2,128]{2,0,1:T(8,128)S(1)}, u32[]{:S(2)}, u32[]{:S(2)}) collective-permute-start(f32[16,2,128]{2,0,1:T(8,128)S(1)} %select_bitcast_fusion.3), channel_id=1, source_target_pairs={{0,16},{1,17},{2,18},{3,19},{4,20},{5,21},{6,22},{7,23},{8,24},{9,... | collective-permute-start | bytes 49160 | tf_op jit(solution)/shard_map/ppermute | solution.py:13
  167.9 2.6 copy-start.1
  249.2 4.6 collective-permute-start.6
  251.8 6.8 %collective-permute-start.7 = (f32[16,2,128]{2,0,1:T(8,128)S(1)}, f32[16,2,128]{2,0,1:T(8,128)S(1)}, u32[]{:S(2)}, u32[]{:S(2)}) collective-permute-start(f32[16,2,128]{2,0,1:T(8,128)S(1)} %select_bitcast_fusion.2), channel_id=1, source_target_pairs={{0,1},{1,2},{2,3},{3,4},{4,5},{5,6},{6,7},{7,8},{8,9},{9,10},{10,1... | collective-permute-start | bytes 49160 | tf_op jit(solution)/shard_map/ppermute | solution.py:13
  251.8 6.8 %collective-permute-start.8 = (f32[16,2,128]{2,0,1:T(8,128)S(1)}, f32[16,2,128]{2,0,1:T(8,128)S(1)}, u32[]{:S(2)}, u32[]{:S(2)}) collective-permute-start(f32[16,2,128]{2,0,1:T(8,128)S(1)} %select_bitcast_fusion.2), channel_id=1, source_target_pairs={{0,16},{1,17},{2,18},{3,19},{4,20},{5,21},{6,22},{7,23},{8,24},{9,... | collective-permute-start | bytes 49160 | tf_op jit(solution)/shard_map/ppermute | solution.py:13
  259.2 2.6 copy-start.2
  341.1 4.7 collective-permute-start.9
  343.7 6.8 %collective-permute-start.10 = (f32[16,2,128]{2,0,1:T(8,128)S(1)}, f32[16,2,128]{2,0,1:T(8,128)S(1)}, u32[]{:S(2)}, u32[]{:S(2)}) collective-permute-start(f32[16,2,128]{2,0,1:T(8,128)S(1)} %select_bitcast_fusion.1), channel_id=1, source_target_pairs={{0,1},{1,2},{2,3},{3,4},{4,5},{5,6},{6,7},{7,8},{8,9},{9,10},{10,1... | collective-permute-start | bytes 49160 | tf_op jit(solution)/shard_map/ppermute | solution.py:13
  343.7 6.8 %collective-permute-start.11 = (f32[16,2,128]{2,0,1:T(8,128)S(1)}, f32[16,2,128]{2,0,1:T(8,128)S(1)}, u32[]{:S(2)}, u32[]{:S(2)}) collective-permute-start(f32[16,2,128]{2,0,1:T(8,128)S(1)} %select_bitcast_fusion.1), channel_id=1, source_target_pairs={{0,16},{1,17},{2,18},{3,19},{4,20},{5,21},{6,22},{7,23},{8,24},{9,... | collective-permute-start | bytes 49160 | tf_op jit(solution)/shard_map/ppermute | solution.py:13
  351.1 2.6 copy-start.3
  432.5 4.7 collective-permute-start.12
  435.1 6.8 %collective-permute-start.13 = (f32[16,2,128]{2,0,1:T(8,128)S(1)}, f32[16,2,128]{2,0,1:T(8,128)S(1)}, u32[]{:S(2)}, u32[]{:S(2)}) collective-permute-start(f32[16,2,128]{2,0,1:T(8,128)S(1)} %select_bitcast_fusion), channel_id=1, source_target_pairs={{0,1},{1,2},{2,3},{3,4},{4,5},{5,6},{6,7},{7,8},{8,9},{9,10},{10,1... | collective-permute-start | bytes 49160 | tf_op jit(solution)/shard_map/ppermute | solution.py:13
  435.1 6.8 %collective-permute-start.14 = (f32[16,2,128]{2,0,1:T(8,128)S(1)}, f32[16,2,128]{2,0,1:T(8,128)S(1)}, u32[]{:S(2)}, u32[]{:S(2)}) collective-permute-start(f32[16,2,128]{2,0,1:T(8,128)S(1)} %select_bitcast_fusion), channel_id=1, source_target_pairs={{0,16},{1,17},{2,18},{3,19},{4,20},{5,21},{6,22},{7,23},{8,24},{9,... | collective-permute-start | bytes 49160 | tf_op jit(solution)/shard_map/ppermute | solution.py:13
  442.5 2.6 copy-start.4
